TPU v7x, 32 devices: a whole 2x2x4 slice. The times are simulated.
32 devices in a mesh: expert: 8 (over z, core), width: 4 (over y, x).
Axes of the slice: x: 2, y: 2, z: 4, core: 2. Of those that a mesh axis runs over, the one named last changes fastest.
Arguments:
- up_weights: float32 [32, 4096, 1536], P('expert', 'width'), may hold values from -0.2 to 0.2
- fisher: float32 [32, 4096], P('expert', 'width'), may hold values from 0.1 to 10
- factor_left: float32 [32, 4096, 128], P('expert', 'width'), may hold values from -0.09375 to 0.09375
- factor_right: float32 [32, 128, 1536], P('expert'), may hold values from -0.25 to 0.25
- calib_rows: bfloat16 [8192, 4096], P('expert', 'width'), may hold values from -6 to 6
- routes: int32 [8192, 1], P('expert'), may hold values from 0 to 31; in each aligned block of 1024 rows (0 to 1023, 1024 to 2047, ...) at most 64 rows name the same one
Outputs:
- shared_base: float32 [4096, 1536], P('width')
- residual_out: float32 [8192, 1536], P('expert', 'width')
Inputs may be any that keep to these rules, and one draw needn't show every extreme that they name: `routes`: within the rows of one device (each aligned block of 1024 rows) no expert is named by more than 64 rows, a bound that some block reaches.
All inputs are finite; a program needn't handle non-finite values.
Results may differ from a plain program's by a relative error of at most 0.0003.
Values may be sent and summed in bfloat16 or wider, within the bound.
A program may use at most 192 MiB of HBM per device.

v0:
```python
import jax
import jax.numpy as jnp
from jax import lax
from jax.sharding import PartitionSpec as P


def local(up_weights, fisher, factor_left, factor_right, calib_rows, routes):
    exp_local, width_rows, hidden = up_weights.shape
    groups = lax.axis_size("expert")
    expert_total = exp_local * groups
    tok_rows = calib_rows.shape[0]
    capacity = 2 * tok_rows // expert_total
    route_ids = routes[:, 0]
    one_hot = (route_ids[:, None] == jnp.arange(expert_total, dtype=jnp.int32)[None, :]).astype(
        jnp.int32
    )
    earlier_count = jnp.cumsum(one_hot, axis=0) - one_hot
    slot_index = jnp.sum(earlier_count * one_hot, axis=1)
    target = route_ids * capacity + slot_index
    outgoing = (
        jnp.zeros((expert_total * capacity, width_rows), jnp.bfloat16).at[target].set(calib_rows)
    )
    outgoing = outgoing.reshape(groups, exp_local * capacity, width_rows)
    incoming = lax.all_to_all(outgoing, "expert", split_axis=0, concat_axis=0, tiled=True)
    weighted_local = jnp.einsum("ed,edf->df", fisher, up_weights, precision=lax.Precision.HIGHEST)
    total_local = jnp.sum(fisher, axis=0)
    weighted_sum, weight_total = lax.psum((weighted_local, total_local), "expert")
    shared_base = weighted_sum / weight_total[:, None]
    low_rank = jnp.einsum(
        "edr,erf->edf", factor_left, factor_right, precision=lax.Precision.HIGHEST
    )
    residual = up_weights - shared_base[None] - low_rank
    routed_rows = incoming.reshape(groups, exp_local, capacity, width_rows)
    partial_value = jnp.einsum(
        "sejd,edf->sejf", routed_rows.astype(jnp.float32), residual, precision=lax.Precision.HIGHEST
    )
    values = lax.psum_scatter(partial_value, "width", scatter_dimension=3, tiled=True)
    returned = lax.all_to_all(
        values.reshape(groups, exp_local * capacity, values.shape[3]),
        "expert",
        split_axis=0,
        concat_axis=0,
        tiled=True,
    )
    returned = returned.reshape(expert_total * capacity, values.shape[3])
    result = returned[target]
    return (shared_base, result)


def solution(mesh):
    placed = (
        P("expert", "width", None),
        P("expert", "width"),
        P("expert", "width", None),
        P("expert", None, None),
        P("expert", "width"),
        P("expert", None),
    )
    return jax.shard_map(
        local,
        mesh=mesh,
        in_specs=placed,
        out_specs=(P("width", None), P("expert", "width")),
        check_vma=False,
    )
```

profile of v0, /device:TPU:0, one launch (start us, length us, event | category | flops | bytes accessed | tf_op | source)
XLA Modules:
  0.0 508.7 jit_solution(13344220027471497440)
XLA Ops:
  7.2 0.0 copy-start
  7.2 0.8 fusion.16
  8.0 9.0 %reduce-window.6 = s32[32,8,128]{2,1,0:T(8,128)S(1)} reduce-window(s32[32,8,128]{2,1,0:T(8,128)S(1)} %fusion.16, s32[]{:T(128)} %constant.4.clone.1), window={size=1x1x128 pad=0_0x0_0x127_0}, to_apply=%region_3.4 | reduce-window | flops 4161536 | bytes 262148 | tf_op jit(solution)/shard_map/reduce-window
  17.1 0.1 slice.10
  17.1 0.1 copy.8
  17.3 0.1 copy.9
  17.4 0.1 broadcast_add_fusion
  17.5 0.7 fusion.15
  18.2 0.7 compare_select_fusion
  18.9 8.6 %scatter_custom_fusion = bf16[2048,1024]{1,0:T(8,128)(2,1)} fusion(s32[1024]{0:T(1024)S(1)} %bitcast.51, bf16[1024,1024]{1,0:T(8,128)(2,1)} %param.10, bf16[]{:T(256)} %constant.6.clone.1), kind=kCustom, calls=%fused_computation.13 | custom fusion | bytes 4194816 | tf_op jit(solution)/shard_map/scatter | solution.py:21
  27.5 0.0 copy-start.2
  27.5 6.5 %all-to-all-start = ((bf16[8,256,1024]{2,1,0:T(8,128)(2,1)}), bf16[8,256,1024]{2,1,0:T(8,128)(2,1)}, u32[]{:S(2)}, u32[]{:S(2)}) async-start(bf16[8,256,1024]{2,1,0:T(8,128)(2,1)} %bitcast.44), calls=%async_computation | async-start | bytes 8388608 | tf_op jit(solution)/shard_map/all_to_all | solution.py:24
  34.0 0.0 all-reduce.2.cloned.1.call-start
  34.1 0.0 copy-done.2
  34.1 1.0 copy.12
  35.1 66.3 %fusion.2 = f32[1024,1,1536]{2,1,0:T(1,128)S(1)} fusion(f32[4,1024,1]{0,2,1:T(1,128)} %copy.12, f32[4,1024,1536]{2,1,0:T(8,128)} %param.6), kind=kOutput, calls=%fused_computation.4 | convolution fusion | flops 75497472 | bytes 31473664 | tf_op jit(solution)/shard_map/ed,edf->df/dot_general | solution.py:25
  101.4 3.1 copy.23
  104.6 0.0 all-reduce.2.cloned.1.call-update
  104.6 0.0 reduce-scatter.2.cloned.1.call-start
  104.7 17.9 %psum.15 = f32[1024]{0:T(1024)S(1)} all-reduce(f32[1024]{0:T(1024)S(1)} %reduce_sum.20), channel_id=1, replica_groups=mesh['expert'=8,'width'=4] {'expert'}, use_global_device_ids=true, to_apply=%region_2.3 | all-reduce | flops 1024 | bytes 8192 | tf_op jit(solution)/shard_map/psum | solution.py:27
  122.6 0.0 copy-done
  122.6 23.9 %fusion.17 = f32[4,1024,1536]{2,1,0:T(8,128)} fusion(f32[4,1024,128]{2,1,0:T(8,128)} %param.8, f32[4,128,1536]{2,1,0:T(8,128)S(1)} %copy-done), kind=kOutput, calls=%fused_computation.25 | convolution fusion | flops 9663676416 | bytes 30408704 | tf_op jit(solution)/shard_map/edr,erf->edf/dot_general | solution.py:29
  146.5 108.7 %all-reduce.2.cloned.1.call-done = f32[1024,1536]{1,0:T(8,128)} async-done(((f32[1024,1536]{1,0:T(8,128)}), f32[1024,1536]{1,0:T(8,128)}) %all-reduce.2.cloned.1.call-update) | async-done | bytes 6291472 | tf_op jit(solution)/shard_map/psum | solution.py:27
  255.2 6.2 %broadcast_divide_fusion = f32[1024,1536]{1,0:T(8,128)} fusion(f32[1024,1536]{1,0:T(8,128)} %all-reduce.2.cloned.1.call-done, f32[1024]{0:T(1024)S(1)} %psum.15), kind=kLoop, calls=%fused_computation.12 | loop fusion | flops 1572864 | bytes 12587008 | tf_op jit(solution)/shard_map/div | solution.py:28
  261.4 0.0 all-to-all-done
  261.4 32.4 %fusion.7 = f32[8,4,64,1536]{3,2,0,1:T(8,128)} fusion(f32[4,1024,1536]{2,1,0:T(8,128)} %fusion.17, f32[4,1024,1536]{2,1,0:T(8,128)} %param.6, f32[1024,1536]{1,0:T(8,128)} %broadcast_divide_fusion, bf16[8,4,64,1024]{3,2,1,0:T(8,128)(2,1)} %bitcast.11), kind=kOutput, calls=%fused_computation.9 | convolution fusion | flops 38667288576 | bytes 73400320 | tf_op jit(solution)/shard_map/sejd,edf->sejf/dot_general | solution.py:34
  293.9 0.0 reduce-scatter.2.cloned.1.call-update
  293.9 120.8 %reduce-scatter.2.cloned.1.call-done = f32[8,4,64,384]{3,2,0,1:T(8,128)} async-done(((f32[8,4,64,1536]{3,2,0,1:T(8,128)}), f32[8,4,64,384]{3,2,0,1:T(8,128)}) %reduce-scatter.2.cloned.1.call-update) | async-done | bytes 3145744 | tf_op jit(solution)/shard_map/reduce_scatter | solution.py:37
  414.7 3.9 copy.11
  418.6 4.6 all-to-all-start.1
  423.3 71.6 %all-to-all-done.1 = f32[8,256,384]{2,1,0:T(8,128)} async-done(((f32[8,256,384]{2,1,0:T(8,128)}), f32[8,256,384]{2,1,0:T(8,128)}, u32[]{:S(2)}, u32[]{:S(2)}) %all-to-all-start.1) | async-done | bytes 3145760 | tf_op jit(solution)/shard_map/all_to_all | solution.py:38
  494.9 0.0 copy-start.1
  494.9 7.0 %gather_fusion = f32[1024,384]{1,0:T(8,128)} fusion(f32[2048,384]{1,0:T(8,128)} %bitcast.14, s32[1024]{0:T(1024)S(1)} %broadcast_clamp_fusion), kind=kCustom, calls=%fused_computation | custom fusion | bytes 3149824 | tf_op jit(solution)/shard_map/gather | solution.py:46
  501.9 0.0 copy-done.1
  (4 shorter events, 0.1 us)
Async XLA Ops:
  7.2 115.4 %copy-start = (f32[4,128,1536]{2,1,0:T(8,128)S(1)}, f32[4,128,1536]{2,1,0:T(8,128)}, u32[]{:S(2)}) copy-start(f32[4,128,1536]{2,1,0:T(8,128)} %param.9) | copy-start | bytes 9437188
  27.5 6.5 %copy-start.2 = (f32[4,1024]{1,0:T(4,128)S(1)}, f32[4,1024]{1,0:T(4,128)}, u32[]{:S(2)}) copy-start(f32[4,1024]{1,0:T(4,128)} %param.7) | copy-start | bytes 49156
  27.5 233.9 %all-to-all-start = ((bf16[8,256,1024]{2,1,0:T(8,128)(2,1)}), bf16[8,256,1024]{2,1,0:T(8,128)(2,1)}, u32[]{:S(2)}, u32[]{:S(2)}) async-start(bf16[8,256,1024]{2,1,0:T(8,128)(2,1)} %bitcast.44), calls=%async_computation | async-start | bytes 8388608 | tf_op jit(solution)/shard_map/all_to_all | solution.py:24
  34.0 221.1 %all-reduce.2.cloned.1.call-start = ((), (), s32[]{:S(2)}) async-start(), calls=%async_computation.3 | async-start | bytes 12582912 | tf_op jit(solution)/shard_map/psum | solution.py:27
  104.6 310.1 %reduce-scatter.2.cloned.1.call-start = ((), (), s32[]{:S(2)}) async-start(), calls=%async_computation.4 | async-start | bytes 15728640 | tf_op jit(solution)/shard_map/reduce_scatter | solution.py:37
  418.6 76.2 %all-to-all-start.1 = ((f32[8,256,384]{2,1,0:T(8,128)}), f32[8,256,384]{2,1,0:T(8,128)}, u32[]{:S(2)}, u32[]{:S(2)}) async-start(f32[8,256,384]{2,1,0:T(8,128)} %bitcast.13), calls=%async_computation.2 | async-start | bytes 6291456 | tf_op jit(solution)/shard_map/all_to_all | solution.py:38
  494.9 7.0 %copy-start.1 = (f32[4,128,1536]{2,1,0:T(8,128)S(1)}, f32[4,128,1536]{2,1,0:T(8,128)}, u32[]{:S(2)}) copy-start(f32[4,128,1536]{2,1,0:T(8,128)} %param.9) | copy-start | bytes 9437188
Sparse Core Ops, SparseCore 0:
  104.7 150.4 all-reduce.1
  294.0 120.6 reduce-scatter.1
where the time goes:
time: 509 us
  waiting for transfers between devices  301 us (59%)
  matrix products  123 us (24%)
  local copies, waits for them, and re-layouts  24.1 us (5%)
  blocking collectives  17.9 us (4%)
  other arithmetic  17.7 us (3%)
  between operations  14.1 us (3%)
  starting transfers between devices  11.2 us (2%)
    reduce_scatter x1, waiting for transfers between devices, local(): lax.psum_scatter(partial_value, 'width', scatter_dimension=3, tiled=True)  121 us
    psum x1, waiting for transfers between devices, local(): lax.psum((weighted_local, total_local), 'expert')  109 us
    all_to_all x1, waiting for transfers between devices, local(): lax.all_to_all(values.reshape(groups, exp_local * capacity, values.shape[...  71.6 us
    dot_general x1, matrix products, local(): jnp.einsum('ed,edf->df', fisher, up_weights, precision=lax.Precision.HIGH...  66.3 us
    dot_general x1, matrix products, local(): jnp.einsum('sejd,edf->sejf', routed_rows.astype(jnp.float32), residual, p...  32.4 us
    dot_general x1, matrix products, local(): jnp.einsum('edr,erf->edf', factor_left, factor_right, precision=lax.Preci...  23.9 us
    psum x1, blocking collectives, local(): lax.psum((weighted_local, total_local), 'expert')  17.9 us
  transfers between devices with their start and end apart: 4, of which 3 were waited for; matrix products, arithmetic and copies ran while one was open for 20% of the time, Pallas kernels for 0%

commit v1 on v0

v1 whole, which is shorter than its diff:
```python
import functools

import jax
import jax.numpy as jnp
from jax import lax
from jax.experimental import pallas as pl
from jax.experimental.pallas import tpu as pltpu
from jax.sharding import PartitionSpec as P

PAD = 16
CHUNKS = 2


def encode(values, axis):
    top = jnp.max(jnp.abs(values), axis=axis, keepdims=True)
    code = jnp.ceil(jnp.log2(jnp.maximum(top, 1e-30)) * 256.0)
    level = jnp.round(values * (32767.0 * jnp.exp2(code * (-1.0 / 256.0))))
    level = jnp.clip(level, -32767.0, 32767.0)
    return level.astype(jnp.int32).astype(jnp.int16), code.astype(jnp.int32).astype(jnp.int16)


def step_of(code):
    return jnp.exp2(code.astype(jnp.float32) * (1.0 / 256.0)) * (1.0 / 32767.0)


def split(x):
    high = x.astype(jnp.bfloat16)
    return high, (x - high.astype(jnp.float32)).astype(jnp.bfloat16)


def product_kernel(rows_ref, up_ref, base_ref, left_ref, right_ref, out_ref):
    dot = functools.partial(jnp.dot, preferred_element_type=jnp.float32)
    left_high, left_low = split(left_ref[0])
    right_high, right_low = split(right_ref[0])
    low_rank = dot(left_high, right_high) + (dot(left_high, right_low) + dot(left_low, right_high))
    high, low = split(up_ref[0] - base_ref[...] - low_rank)
    groups, _, capacity, width_rows = rows_ref.shape
    rows = rows_ref[...].reshape(groups * capacity, width_rows)
    value = dot(rows, high) + dot(rows, low)
    level, code = encode(value, 0)
    out_ref[0, 0, : groups * capacity, :] = level
    out_ref[0, 0, groups * capacity :, :] = jnp.broadcast_to(code.astype(jnp.int32), (PAD, value.shape[1])).astype(jnp.int16)


def product(rows, up, base, left, right, first, parts):
    groups, count, capacity, width_rows = rows.shape
    hidden = up.shape[2]
    rank = left.shape[2]
    block = hidden // parts
    if block % 128:
        parts, block = 1, hidden
    total = groups * capacity
    return pl.pallas_call(
        product_kernel,
        grid=(count, parts),
        in_specs=[
            pl.BlockSpec((groups, 1, capacity, width_rows), lambda e, f: (0, e, 0, 0)),
            pl.BlockSpec((1, width_rows, block), lambda e, f: (first + e, 0, f)),
            pl.BlockSpec((width_rows, block), lambda e, f: (0, f)),
            pl.BlockSpec((1, width_rows, rank), lambda e, f: (first + e, 0, 0)),
            pl.BlockSpec((1, rank, block), lambda e, f: (first + e, 0, f)),
        ],
        out_specs=pl.BlockSpec((1, 1, total + PAD, block), lambda e, f: (f, e, 0, 0)),
        out_shape=jax.ShapeDtypeStruct((parts, count, total + PAD, block), jnp.int16),
        cost_estimate=pl.CostEstimate(
            flops=4 * count * total * width_rows * hidden,
            bytes_accessed=count * (8 * width_rows * hidden + 2 * total * (width_rows + hidden)),
            transcendentals=0,
        ),
        name="product",
    )(rows, up, base, left, right)


def local(up_weights, fisher, factor_left, factor_right, calib_rows, routes):
    exp_local, width_rows, hidden = up_weights.shape
    groups = lax.axis_size("expert")
    parts = lax.axis_size("width")
    expert_total = exp_local * groups
    tok_rows = calib_rows.shape[0]
    capacity = 2 * tok_rows // expert_total
    slots = expert_total * capacity
    block = hidden // parts

    total_local = jnp.sum(fisher, axis=0)
    weighted = fisher[0][:, None] * up_weights[0]
    for e in range(1, exp_local):
        weighted = weighted + fisher[e][:, None] * up_weights[e]
    weight_total = lax.psum_scatter(total_local, "expert", scatter_dimension=0, tiled=True)
    shard = lax.psum_scatter(weighted, "expert", scatter_dimension=0, tiled=True)
    shard = shard / weight_total[:, None]
    level, code = encode(shard, 0)
    packed = jnp.concatenate([level, jnp.broadcast_to(code, (PAD, hidden))], axis=0)
    packed = lax.all_gather(packed, "expert", axis=0)
    keep = shard.shape[0]
    shared_base = packed[:, :keep].astype(jnp.float32) * step_of(packed[:, keep : keep + 1])
    shared_base = shared_base.reshape(width_rows, hidden)

    route_ids = routes[:, 0]
    one_hot = route_ids[:, None] == jnp.arange(expert_total, dtype=jnp.int32)[None, :]
    before = jnp.arange(tok_rows)[:, None] > jnp.arange(tok_rows)[None, :]
    earlier = jnp.dot(
        before.astype(jnp.bfloat16), one_hot.astype(jnp.bfloat16), preferred_element_type=jnp.float32
    )
    slot_index = jnp.sum(jnp.where(one_hot, earlier, 0.0), axis=1).astype(jnp.int32)
    step = exp_local // CHUNKS
    target = route_ids * capacity + slot_index
    owner, inner = route_ids // exp_local, route_ids % exp_local

    returned = []
    for c in range(CHUNKS):
        first = c * step
        place = jnp.arange(groups * step * capacity, dtype=jnp.int32)
        spot = (place // (step * capacity)) * (exp_local * capacity) + first * capacity + place % (step * capacity)
        chosen = (spot[:, None] == target[None, :]).astype(jnp.bfloat16)
        outgoing = jnp.dot(chosen, calib_rows, preferred_element_type=jnp.float32).astype(jnp.bfloat16)
        outgoing = outgoing.reshape(groups, step * capacity, width_rows)
        incoming = lax.all_to_all(outgoing, "expert", split_axis=0, concat_axis=0, tiled=True)
        incoming = incoming.reshape(groups, step, capacity, width_rows)
        value = product(incoming, up_weights, shared_base, factor_left, factor_right, first, parts)
        if value.shape[0] != parts:
            value = value[0].reshape(step, -1, parts, block).transpose(2, 0, 1, 3)
        value = lax.all_to_all(value, "width", split_axis=0, concat_axis=0, tiled=True)
        rows_all = groups * capacity
        summed = jnp.sum(
            value[:, :, :rows_all].astype(jnp.float32) * step_of(value[:, :, rows_all : rows_all + 1]), axis=0
        )
        summed = summed.reshape(step, groups, capacity, block).transpose(1, 0, 2, 3)
        summed = summed.reshape(groups, step * capacity, block)
        level, code = encode(summed, 1)
        back = jnp.concatenate([level, jnp.broadcast_to(code, (groups, PAD, block))], axis=1)
        back = lax.all_to_all(back, "expert", split_axis=0, concat_axis=0, tiled=True)
        home = back[:, : step * capacity].astype(jnp.float32) * step_of(back[:, step * capacity : step * capacity + 1])
        returned.append(home.reshape(groups * step * capacity, block))
    returned = jnp.concatenate(returned, axis=0)
    chunk, within = inner // step, inner % step
    where = ((chunk * groups + owner) * step + within) * capacity + slot_index
    return (shared_base, returned[where])


def solution(mesh):
    placed = (
        P("expert", "width", None),
        P("expert", "width"),
        P("expert", "width", None),
        P("expert", None, None),
        P("expert", "width"),
        P("expert", None),
    )
    return jax.shard_map(
        local,
        mesh=mesh,
        in_specs=placed,
        out_specs=(P("width", None), P("expert", "width")),
        check_vma=False,
    )
```

time: 509 us -> 401 us (0.79)
  waiting for transfers between devices: 301 us -> 103 us
  blocking collectives: 17.9 us -> 156 us
  matrix products: 123 us -> 7.98 us
  Pallas kernels: 0 us -> 42.3 us
  starting transfers between devices: 11.2 us -> 31.9 us
  other arithmetic: 17.7 us -> 32.1 us
  local copies, waits for them, and re-layouts: 24.1 us -> 11.8 us
    dot_general x3, matrix products: 123 us -> 7.98 us  [the longest x2 7.45 us: local(): jnp.dot(chosen, calib_rows, preferred_element_type=jnp.float32)]
    psum x1 -> x0, waiting for transfers between devices: 109 us -> none  [local(): lax.psum((weighted_local, total_local), 'expert')]
    reduce_scatter x1, waiting for transfers between devices: 121 us -> 14.8 us  [local(): lax.psum_scatter(weighted, 'expert', scatter_dimension=0, tiled=True)]
    unnamed x0 -> x1, blocking collectives: none -> 79.2 us
    all_gather x0 -> x1, blocking collectives: none -> 76.7 us  [local(): packed = lax.all_gather(packed, 'expert', axis=0)]
    pallas_call x0 -> x2, Pallas kernels: none -> 42.3 us  [product(): pl.pallas_call(product_kernel, grid=(count, parts), in_specs=[pl.BlockSpe...]
    psum x1 -> x0, blocking collectives: 17.9 us -> none  [local(): lax.psum((weighted_local, total_local), 'expert')]
    all_to_all x1 -> x4, waiting for transfers between devices: 71.6 us -> 88.3 us  [the longest x2 48.2 us: local(): lax.all_to_all(value, 'width', split_axis=0, concat_axis=0, tiled=True)]
  transfers between devices with their start and end apart: 4 -> 7, of which waited for: 3 -> 5; matrix products, arithmetic and copies ran while one was open for 20% -> 6% of each run, Pallas kernels for 0% -> 11%
where the time goes in v1:
time: 401 us; the launch traced here: 400 us
  blocking collectives  156 us (39%)
  waiting for transfers between devices  103 us (26%)
  Pallas kernels  42.3 us (11%)
  other arithmetic  32.1 us (8%)
  starting transfers between devices  31.9 us (8%)
  between operations  15 us (4%)
  local copies, waits for them, and re-layouts  11.8 us (3%)
  matrix products  7.98 us (2%)
    unnamed x1, blocking collectives  79.2 us
    all_gather x1, blocking collectives, local(): packed = lax.all_gather(packed, 'expert', axis=0)  76.7 us
    all_to_all x2, waiting for transfers between devices, local(): lax.all_to_all(value, 'width', split_axis=0, concat_axis=0, tiled=True)  48.2 us
    pallas_call x2, Pallas kernels, product(): pl.pallas_call(product_kernel, grid=(count, parts), in_specs=[pl.BlockSpe...  42.3 us
    all_to_all x2, waiting for transfers between devices, local(): lax.all_to_all(back, 'expert', split_axis=0, concat_axis=0, tiled=True)  40.1 us
    all_to_all x2, starting transfers between devices, local(): lax.all_to_all(outgoing, 'expert', split_axis=0, concat_axis=0, tiled=True)  15.2 us
    reduce_scatter x1, waiting for transfers between devices, local(): lax.psum_scatter(weighted, 'expert', scatter_dimension=0, tiled=True)  14.8 us
    add x1, other arithmetic, local(): weighted = weighted + fisher[e][:, None] * up_weights[e]  12.1 us
  transfers between devices with their start and end apart: 7, of which 5 were waited for; matrix products, arithmetic and copies ran while one was open for 6% of the time, Pallas kernels for 11%

profile of v1, /device:TPU:0, one launch (start us, length us, event | category | flops | bytes accessed | tf_op | source)
XLA Modules:
  0.0 400.1 jit_solution(9758197784155825715)
XLA Ops:
  7.2 0.0 copy-start
  7.2 0.0 reduce-scatter.2.cloned.1.call-start
  7.2 0.9 fusion.47
  8.2 12.1 %fusion = f32[1024,1536]{1,0:T(8,128)} fusion(f32[4,1024,1536]{2,1,0:T(8,128)} %up_ref.3, f32[1024]{0:T(1024)S(1)} %bitcast.95, f32[1024]{0:T(1024)S(1)} %bitcast.93, f32[1024]{0:T(1024)S(1)} %bitcast.94, f32[1024]{0:T(1024)S(1)} %bitcast.92), kind=kLoop, calls=%fused_computation.2 | loop fusion | flops 11010048 | bytes 31473664 | tf_op jit(solution)/shard_map/add | solution.py:87
  20.2 0.0 copy-start.6
  20.2 0.0 reduce-scatter.2.cloned.1.call-update
  20.3 0.6 copy-done.6
  20.9 0.5 fusion.27
  21.5 0.0 copy-done
  21.5 3.7 fusion.12
  25.2 0.0 copy-start.5
  25.2 0.0 copy-start.7
  25.2 6.5 %all-to-all-start = ((bf16[8,128,1024]{2,1,0:T(8,128)(2,1)}), bf16[8,128,1024]{2,1,0:T(8,128)(2,1)}, u32[]{:S(2)}, u32[]{:S(2)}) async-start(bf16[8,128,1024]{2,1,0:T(8,128)(2,1)} %bitcast.89), calls=%async_computation.1 | async-start | bytes 4194304 | tf_op jit(solution)/shard_map/all_to_all | solution.py:117
  31.7 0.0 copy-done.5
  31.7 0.0 copy-done.7
  31.7 0.6 dynamic-slice
  33.0 79.2 %all-reduce = f32[1024]{0:T(1024)S(1)} all-reduce(f32[1024]{0:T(1024)S(1)} %reduce_sum.36), channel_id=4, replica_groups=mesh['expert'=8,'width'=4] {'expert'}, use_global_device_ids=true, to_apply=%region_2.0.clone | all-reduce | flops 1024 | bytes 8192
  112.1 0.1 dynamic-slice.1
  112.2 3.7 fusion.15
  116.0 14.8 %reduce-scatter.2.cloned.1.call-done = f32[128,1536]{1,0:T(8,128)} async-done(((f32[1024,1536]{1,0:T(8,128)}), f32[128,1536]{1,0:T(8,128)}) %reduce-scatter.2.cloned.1.call-update) | async-done | bytes 786448 | tf_op jit(solution)/shard_map/reduce_scatter | solution.py:89
  130.7 0.0 copy-start.4
  130.7 1.3 abs_reduce_fusion.2
  132.1 0.0 all-to-all-done
  132.1 8.7 %all-to-all-start.3 = ((bf16[8,128,1024]{2,1,0:T(8,128)(2,1)}), bf16[8,128,1024]{2,1,0:T(8,128)(2,1)S(1)}, u32[]{:S(2)}, u32[]{:S(2)}) async-start(bf16[8,128,1024]{2,1,0:T(8,128)(2,1)} %bitcast.88), calls=%async_computation.4 | async-start | bytes 4194304 | tf_op jit(solution)/shard_map/all_to_all | solution.py:117
  140.8 0.0 copy-done.4
  140.8 0.2 convert_convert_fusion
  141.1 76.7 %all-gather.2 = s16[1152,1536]{1,0:T(8,128)(2,1)S(1)} all-gather(s16[144,1536]{1,0:T(8,128)(2,1)S(1)} %pad_add_fusion.2), channel_id=2, replica_groups=mesh['expert'=8,'width'=4] {'expert'}, dimensions={0}, use_global_device_ids=true | all-gather | bytes 3981312 | tf_op jit(solution)/shard_map/all_gather | solution.py:93
  217.9 3.8 convert_multiply_fusion
  221.6 21.1 %product.2 = s16[4,2,528,384]{3,2,1,0:T(8,128)(2,1)} custom-call(bf16[8,2,64,1024]{3,2,1,0:T(8,128)(2,1)} %bitcast.13.rows_ref, f32[4,1024,1536]{2,1,0:T(8,128)} %up_ref.3, f32[1024,1536]{1,0:T(8,128)} %bitcast.76, f32[4,1024,128]{2,1,0:T(8,128)} %left_ref.3, f32[4,128,1536]{2,1,0:T(8,128)} %right_ref.3), custom_call_target="tpu_custom_call" | custom-call | flops 6442450944 | bytes 30408704 | tf_op jit(solution)/shard_map/product/pallas_call | solution.py:53
  242.7 0.0 all-to-all-done.3
  242.7 0.0 copy-start.2
  242.7 1.3 copy-done.2
  244.0 4.9 %all-to-all-start.1 = ((s16[4,2,528,384]{3,2,1,0:T(8,128)(2,1)}), s16[4,2,528,384]{3,2,1,0:T(8,128)(2,1)}, u32[]{:S(2)}, u32[]{:S(2)}) async-start(s16[4,2,528,384]{3,2,1,0:T(8,128)(2,1)} %product.2), calls=%async_computation.2 | async-start | bytes 6488064 | tf_op jit(solution)/shard_map/all_to_all | solution.py:122
  248.9 21.2 %product.3 = s16[4,2,528,384]{3,2,1,0:T(8,128)(2,1)} custom-call(bf16[8,2,64,1024]{3,2,1,0:T(8,128)(2,1)} %bitcast.85, f32[4,1024,1536]{2,1,0:T(8,128)} %up_ref.3, f32[1024,1536]{1,0:T(8,128)} %bitcast.77, f32[4,1024,128]{2,1,0:T(8,128)} %left_ref.3, f32[4,128,1536]{2,1,0:T(8,128)} %right_ref.3), custom_call_target="tpu_custom_call" | custom-call | flops 6442450944 | bytes 30408704 | tf_op jit(solution)/shard_map/product/pallas_call | solution.py:53
  270.1 16.6 %all-to-all-done.1 = s16[4,2,528,384]{3,2,1,0:T(8,128)(2,1)} async-done(((s16[4,2,528,384]{3,2,1,0:T(8,128)(2,1)}), s16[4,2,528,384]{3,2,1,0:T(8,128)(2,1)}, u32[]{:S(2)}, u32[]{:S(2)}) %all-to-all-start.1) | async-done | bytes 3244064 | tf_op jit(solution)/shard_map/all_to_all | solution.py:122
  286.8 4.7 %all-to-all-start.4 = ((s16[4,2,528,384]{3,2,1,0:T(8,128)(2,1)}), s16[4,2,528,384]{3,2,1,0:T(8,128)(2,1)}, u32[]{:S(2)}, u32[]{:S(2)}) async-start(s16[4,2,528,384]{3,2,1,0:T(8,128)(2,1)} %product.3), calls=%async_computation.5 | async-start | bytes 6488064 | tf_op jit(solution)/shard_map/all_to_all | solution.py:122
  291.5 0.8 fusion.34
  292.3 3.3 multiply_reduce_fusion.1
  295.6 0.1 copy.25
  295.7 0.1 abs_reduce_fusion.1
  295.9 0.2 fusion.25
  296.1 1.0 pad_add_fusion
  297.2 31.5 %all-to-all-done.4 = s16[4,2,528,384]{3,2,1,0:T(8,128)(2,1)} async-done(((s16[4,2,528,384]{3,2,1,0:T(8,128)(2,1)}), s16[4,2,528,384]{3,2,1,0:T(8,128)(2,1)}, u32[]{:S(2)}, u32[]{:S(2)}) %all-to-all-start.4) | async-done | bytes 3244064 | tf_op jit(solution)/shard_map/all_to_all | solution.py:122
  328.7 3.6 all-to-all-start.2
  332.2 0.8 fusion.31
  333.1 3.3 multiply_reduce_fusion
  336.4 0.1 copy.27
  336.5 0.1 abs_reduce_fusion
  336.7 0.2 fusion.21
  336.9 1.0 pad_add_fusion.1
  337.9 17.3 %all-to-all-done.2 = s16[8,144,384]{2,1,0:T(8,128)(2,1)S(1)} async-done(((s16[8,144,384]{2,1,0:T(8,128)(2,1)}), s16[8,144,384]{2,1,0:T(8,128)(2,1)S(1)}, u32[]{:S(2)}, u32[]{:S(2)}) %all-to-all-start.2) | async-done | bytes 884768 | tf_op jit(solution)/shard_map/all_to_all | solution.py:131
  355.2 3.6 all-to-all-start.5
  358.8 0.1 compare_select_fusion
  358.9 22.8 %all-to-all-done.5 = s16[8,144,384]{2,1,0:T(8,128)(2,1)S(1)} async-done(((s16[8,144,384]{2,1,0:T(8,128)(2,1)}), s16[8,144,384]{2,1,0:T(8,128)(2,1)S(1)}, u32[]{:S(2)}, u32[]{:S(2)}) %all-to-all-start.5) | async-done | bytes 884768 | tf_op jit(solution)/shard_map/all_to_all | solution.py:131
  381.8 0.0 copy-start.3
  381.8 0.9 copy-done.3
  382.7 0.3 convert_multiply_fusion.2
  383.0 1.4 convert_multiply_fusion.1
  384.4 1.9 pad_maximum_fusion
  386.2 0.0 copy-start.1
  386.2 7.0 %gather_fusion = f32[1024,384]{1,0:T(8,128)} fusion(f32[2048,384]{1,0:T(8,128)} %pad_maximum_fusion, s32[1024]{0:T(1024)S(1)} %broadcast_clamp_fusion), kind=kCustom, calls=%fused_computation | custom fusion | bytes 3149824 | tf_op jit(solution)/shard_map/gather | solution.py:137
  393.2 0.0 copy-done.1
  (20 shorter events, 0.3 us)
Async XLA Ops:
  7.2 14.3 %copy-start = (bf16[1024,1024]{1,0:T(8,128)(2,1)S(1)}, bf16[1024,1024]{1,0:T(8,128)(2,1)}, u32[]{:S(2)}) copy-start(bf16[1024,1024]{1,0:T(8,128)(2,1)} %param.10) | copy-start | bytes 6291460
  7.2 123.5 %reduce-scatter.2.cloned.1.call-start = ((), (), s32[]{:S(2)}) async-start(), calls=%async_computation.7 | async-start | bytes 7077888 | tf_op jit(solution)/shard_map/reduce_scatter | solution.py:89
  20.2 0.7 copy-start.6
  25.2 6.5 %copy-start.5 = (f32[4,1024]{1,0:T(4,128)S(1)}, f32[4,1024]{1,0:T(4,128)}, u32[]{:S(2)}) copy-start(f32[4,1024]{1,0:T(4,128)} %param.7) | copy-start | bytes 49156
  25.2 6.5 %copy-start.7 = (u32[32]{0:T(128)S(1)}, u32[32]{0:T(128)}, u32[]{:S(2)}) copy-start(u32[32]{0:T(128)} %constant.136) | copy-start | bytes 388
  25.2 106.9 %all-to-all-start = ((bf16[8,128,1024]{2,1,0:T(8,128)(2,1)}), bf16[8,128,1024]{2,1,0:T(8,128)(2,1)}, u32[]{:S(2)}, u32[]{:S(2)}) async-start(bf16[8,128,1024]{2,1,0:T(8,128)(2,1)} %bitcast.89), calls=%async_computation.1 | async-start | bytes 4194304 | tf_op jit(solution)/shard_map/all_to_all | solution.py:117
  130.7 10.1 %copy-start.4 = (f32[128,1536]{1,0:T(8,128)S(1)}, f32[128,1536]{1,0:T(8,128)}, u32[]{:S(2)}) copy-start(f32[128,1536]{1,0:T(8,128)} %reduce-scatter.2.cloned.1.call-done) | copy-start | bytes 2359300
  132.1 110.6 %all-to-all-start.3 = ((bf16[8,128,1024]{2,1,0:T(8,128)(2,1)}), bf16[8,128,1024]{2,1,0:T(8,128)(2,1)S(1)}, u32[]{:S(2)}, u32[]{:S(2)}) async-start(bf16[8,128,1024]{2,1,0:T(8,128)(2,1)} %bitcast.88), calls=%async_computation.4 | async-start | bytes 4194304 | tf_op jit(solution)/shard_map/all_to_all | solution.py:117
  242.7 1.3 copy-start.2
  244.0 42.7 %all-to-all-start.1 = ((s16[4,2,528,384]{3,2,1,0:T(8,128)(2,1)}), s16[4,2,528,384]{3,2,1,0:T(8,128)(2,1)}, u32[]{:S(2)}, u32[]{:S(2)}) async-start(s16[4,2,528,384]{3,2,1,0:T(8,128)(2,1)} %product.2), calls=%async_computation.2 | async-start | bytes 6488064 | tf_op jit(solution)/shard_map/all_to_all | solution.py:122
  286.8 41.9 %all-to-all-start.4 = ((s16[4,2,528,384]{3,2,1,0:T(8,128)(2,1)}), s16[4,2,528,384]{3,2,1,0:T(8,128)(2,1)}, u32[]{:S(2)}, u32[]{:S(2)}) async-start(s16[4,2,528,384]{3,2,1,0:T(8,128)(2,1)} %product.3), calls=%async_computation.5 | async-start | bytes 6488064 | tf_op jit(solution)/shard_map/all_to_all | solution.py:122
  328.7 26.5 %all-to-all-start.2 = ((s16[8,144,384]{2,1,0:T(8,128)(2,1)}), s16[8,144,384]{2,1,0:T(8,128)(2,1)S(1)}, u32[]{:S(2)}, u32[]{:S(2)}) async-start(s16[8,144,384]{2,1,0:T(8,128)(2,1)} %pad_add_fusion), calls=%async_computation.3 | async-start | bytes 1769472 | tf_op jit(solution)/shard_map/all_to_all | solution.py:131
  355.2 26.5 %all-to-all-start.5 = ((s16[8,144,384]{2,1,0:T(8,128)(2,1)}), s16[8,144,384]{2,1,0:T(8,128)(2,1)S(1)}, u32[]{:S(2)}, u32[]{:S(2)}) async-start(s16[8,144,384]{2,1,0:T(8,128)(2,1)} %pad_add_fusion.1), calls=%async_computation.6 | async-start | bytes 1769472 | tf_op jit(solution)/shard_map/all_to_all | solution.py:131
  381.8 0.9 copy-start.3
  386.2 7.0 %copy-start.1 = (bf16[1024,1024]{1,0:T(8,128)(2,1)S(1)}, bf16[1024,1024]{1,0:T(8,128)(2,1)}, u32[]{:S(2)}) copy-start(bf16[1024,1024]{1,0:T(8,128)(2,1)} %param.10) | copy-start | bytes 6291460
Sparse Core Ops, SparseCore 0:
  20.4 110.2 reduce-scatter.1
